TPU v7x, 128 devices: a whole 4x4x4 slice. The times are simulated.
128 devices in a mesh: row: 16 (over x, y), col: 8 (over z, core).
Axes of the slice: x: 4, y: 4, z: 4, core: 2. Of those that a mesh axis runs over, the one named last changes fastest.
Arguments:
- features: float32 [32768, 256], P(('row', 'col')), may hold values from -6 to 6
- new_features: float32 [8192, 256], P(('row', 'col')), may hold values from -6 to 6
- lengths: int32 [32768], P(('row', 'col')), may hold values from 1 to 64
- targets: float32 [32768, 64], P(('row', 'col')), may hold values from -6 to 6
- prior_train: float32 [32768, 256], P(('row', 'col')), may hold values from -6 to 6
- noise_draw: float32 [32768, 256], P(('row', 'col')), may hold values from -6 to 6
- prior_new: float32 [8192, 256], P(('row', 'col')), may hold values from -6 to 6
- time_kernel: float32 [64, 64], replicated, may hold values from -16 to 16.5, as said below
- noise_var: float32 [64], replicated, may hold values from 0.05 to 0.5
Outputs:
- residual: float32 [32768, 256], P(('row', 'col'))
- predicted: float32 [8192, 256], P(('row', 'col'))
Inputs may be any that keep to these rules, and one draw needn't show every extreme that they name: `time_kernel`: symmetric positive definite.
All inputs are finite; a program needn't handle non-finite values.
Results may differ from a plain program's by a relative error of at most 0.00022.
Values sent between devices are 32-bit elements; how exact they have to be, the bound alone decides.
No kernel may reach another device: no remote copies, remote signals or barrier semaphores. Data moves between devices by JAX's collectives and lax.ppermute only.
A program may use at most 128 MiB of HBM per device.

v0:
```python
import jax
import jax.numpy as jnp
import numpy as np
from jax import lax
from jax.experimental import pallas as pl
from jax.experimental.pallas import tpu as pltpu
from jax.sharding import PartitionSpec as P


AXES = ("row", "col")
F32 = jnp.float32
BF16 = jnp.bfloat16


def index(x, y, z, core):
    return ((x % 4) * 4 + y % 4) * 8 + (z % 4) * 2 + core % 2


def shift(values, dx=0, dy=0, dz=0, core=0):
    pairs = [
        (index(x, y, z, k), index(x + dx, y + dy, z + dz, k + core))
        for x in range(4)
        for y in range(4)
        for z in range(4)
        for k in range(2)
    ]
    return lax.ppermute(values, AXES, pairs)


def ring(values, axis):
    half = values.shape[0] // 2
    below = shift(values, **{axis: 1})
    above = shift(values, **{axis: -1})
    first = shift(below[:half], **{axis: 1})
    second = shift(above[half:], **{axis: -1})
    return [values, below, above, first, second]


def join_kernel(*refs):
    start = 0
    for ref in refs[:-1]:
        refs[-1][start : start + ref.shape[0], :] = ref[...]
        start += ref.shape[0]


def join(parts):
    rows = sum(part.shape[0] for part in parts)
    return pl.pallas_call(
        join_kernel,
        out_shape=jax.ShapeDtypeStruct((rows, parts[0].shape[1]), F32),
        name="join",
    )(*parts)


def plane_half(values, near, far):
    return ring(join(ring(values, near)), far)


def plane_gather(values):
    middle = values.shape[0] // 2
    return [plane_half(values[:middle], "dx", "dy"), plane_half(values[middle:], "dy", "dx")]


OFFSETS = (0, -1, 1, 2)


def at(table, axis):
    return lax.dynamic_index_in_dim(jnp.asarray(table), lax.axis_index(axis), keepdims=False)


def plane_order():
    steps = [(near, far) for far in OFFSETS for near in OFFSETS]
    table = []
    for x in range(4):
        for y in range(4):
            one = [((x + near) % 4 * 4 + (y + far) % 4) * 2 for near, far in steps]
            two = [((x + far) % 4 * 4 + (y + near) % 4) * 2 + 1 for near, far in steps]
            table.append(one + two)
    return at(np.array(table, np.int32), "row")


def line_order(other):
    table = [
        [(z + step) % 4 * 2 + (core + other) % 2 for step in OFFSETS]
        for z in range(4)
        for core in range(2)
    ]
    return at(np.array(table, np.int32), "col")


def split(values):
    high = values.astype(BF16)
    return high, (values - high.astype(F32)).astype(BF16)


def dot(first, second, dims=(((1,), (0,)), ((), ()))):
    return lax.dot_general(first, second, dims, preferred_element_type=F32)


def dot_split(first, second, dims=(((1,), (0,)), ((), ()))):
    return dot(first[0], second[0], dims) + (
        dot(first[0], second[1], dims) + dot(first[1], second[0], dims)
    )


def form_kernel(n, order, *refs):
    cols, rows, high_out, low_out, high_cols, low_cols, high_rows, low_rows = refs[:n], *refs[n:]
    step = pl.program_id(0)

    @pl.when(step == 0)
    def _():
        start = 0
        for ref in cols:
            high, low = split(ref[...])
            high_cols[start : start + ref.shape[0], :] = high
            low_cols[start : start + ref.shape[0], :] = low
            start += ref.shape[0]
        size = rows.shape[1]
        for i in range(4):
            high, low = split(rows[order[i]])
            high_rows[i * size : (i + 1) * size, :] = high
            low_rows[i * size : (i + 1) * size, :] = low

    width = high_out.shape[1]
    here = pl.ds(pl.multiple_of(step * width, width), width)
    cols_here = (high_cols[here, :], low_cols[here, :])
    size = high_out.shape[0] // 4
    for i in range(4):
        rows_here = slice(i * size, (i + 1) * size)
        inner = dot_split(
            (high_rows[rows_here, :], low_rows[rows_here, :]),
            cols_here,
            (((1,), (1,)), ((), ())),
        )
        high, low = split(inner + inner * inner * inner)
        high_out[rows_here, :] = high
        low_out[rows_here, :] = low


def whole(part):
    return pl.BlockSpec(part.shape, lambda i, *_: (0,) * part.ndim)


def form(order, rows, cols, block):
    width = sum(part.shape[0] for part in cols)
    total, depth = 4 * rows.shape[1], rows.shape[2]
    tile = pl.BlockSpec((total, block), lambda i, *_: (0, i))
    return pl.pallas_call(
        lambda *refs: form_kernel(len(cols), *refs),
        grid_spec=pltpu.PrefetchScalarGridSpec(
            num_scalar_prefetch=1,
            grid=(width // block,),
            in_specs=[whole(part) for part in [*cols, rows]],
            out_specs=[tile, tile],
            scratch_shapes=[pltpu.VMEM((width, depth), BF16)] * 2
            + [pltpu.VMEM((total, depth), BF16)] * 2,
        ),
        out_shape=[jax.ShapeDtypeStruct((total, width), BF16)] * 2,
        cost_estimate=pl.CostEstimate(
            flops=6 * total * width * depth, bytes_accessed=4 * total * width, transcendentals=0
        ),
        name="form",
    )(order, *cols, rows)


def apply_kernel(n, add, order, values, *refs):
    if add:
        before, refs = refs[0], refs[1:]
    tests, high_tile, low_tile, out, sums = refs[:n], *refs[n:]
    step = pl.program_id(0)
    count = high_tile.shape[1] // values.shape[1]
    part = jnp.concatenate([values[order[step * count + i]] for i in range(count)], axis=0)
    result = dot_split((high_tile[...], low_tile[...]), split(part))

    @pl.when(step == 0)
    def _():
        out[...] = result + before[...] if add else result

    @pl.when(step > 0)
    def _():
        out[...] += result

    @pl.when(step == pl.num_programs(0) - 1)
    def _():
        sums[...] = jnp.zeros_like(sums)
        for j, test in enumerate(tests):
            size, block = test.shape[0] // 4, out.shape[0] // 4
            for i in range(4):
                product = test[i * size : (i + 1) * size, :] * out[i * block : i * block + size, :]
                sums[j : j + 1, :] += jnp.sum(product, axis=0, keepdims=True)


def apply(tile, block, order, values, tests=(), before=None, start=0):
    total, columns = tile[0].shape[0], values.shape[2]
    width = order.shape[0] * values.shape[1]
    tiles = pl.BlockSpec((total, block), lambda i, *_: (0, start // block + i))
    operands = [values] + ([] if before is None else [before]) + list(tests)
    out_shape = [
        jax.ShapeDtypeStruct((total, columns), F32),
        jax.ShapeDtypeStruct((8, columns), F32),
    ]
    return pl.pallas_call(
        lambda *refs: apply_kernel(len(tests), before is not None, *refs),
        grid_spec=pltpu.PrefetchScalarGridSpec(
            num_scalar_prefetch=1,
            grid=(width // block,),
            in_specs=[whole(part) for part in operands] + [tiles, tiles],
            out_specs=[whole(part) for part in out_shape],
        ),
        out_shape=out_shape,
        cost_estimate=pl.CostEstimate(
            flops=6 * total * width * columns, bytes_accessed=4 * total * width, transcendentals=0
        ),
        name="apply",
    )(order, *operands, *tile)


def total_sums(partial, samples):
    devices = lax.axis_size("row") * lax.axis_size("col")
    spread = jnp.broadcast_to(partial[None], (devices,) + partial.shape)
    sums = jnp.sum(lax.all_to_all(spread, AXES, 0, 0), axis=0)
    return jnp.sum(sums.reshape(partial.shape[0], samples, -1), axis=2)


def shards(
    features,
    new_features,
    lengths,
    targets,
    prior_train,
    noise_draw,
    prior_new,
    time_kernel,
    noise_var,
):
    checkpoints = time_kernel.shape[0]
    columns = prior_train.shape[1]
    samples = columns // checkpoints
    items = features.shape[0]
    block = items + new_features.shape[0]

    both = jnp.concatenate([features, new_features], axis=0)
    normed = both / jnp.sqrt(jnp.sum(both * both, axis=1, keepdims=True) + 1e-06)

    line = lax.axis_size("col")
    rows = lax.all_to_all(jnp.broadcast_to(normed[None], (line,) + normed.shape), "col", 0, 0)
    cols = [part for half in plane_gather(normed[:items]) for part in half]
    middle = block // 2

    mixing = jnp.kron(jnp.eye(samples, dtype=F32), time_kernel)

    def mix(values):
        return jnp.dot(values, mixing, precision=lax.Precision.HIGHEST)

    position = jnp.arange(columns, dtype=jnp.int32) % checkpoints
    mask = (position[None, :] < lengths[:, None]).astype(F32)
    noise_cols = jnp.tile(noise_var, samples)
    rhs = mask * (jnp.tile(targets, (1, samples)) - prior_train - jnp.sqrt(noise_cols) * noise_draw)
    plane = lax.axis_size("row")
    order = plane_order()
    half = items // 2

    def exchange(values):
        spread_out = jnp.broadcast_to(values[None], (plane,) + values.shape)
        received = lax.all_to_all(spread_out, "row", 0, 0)
        return received.reshape(-1, half, columns)

    def line_gather(values):
        own = join(ring(values, "dz"))
        return own, shift(own, core=1)

    def reduce_rows(own, other):
        received = shift(other, core=1)
        own, below, above, opposite = jnp.split(own + received, 4)
        up = shift(opposite[:middle], dz=1)
        down = shift(opposite[middle:], dz=-1)
        above = jnp.concatenate([above[:middle] + up, above[middle:]], axis=0)
        below = jnp.concatenate([below[:middle], below[middle:] + down], axis=0)
        own = own + (shift(above, dz=1) + shift(below, dz=-1))
        return own[:items], own[items:]

    def spread(scalars):
        return jnp.repeat(scalars, checkpoints)[None, :]

    def local_sums(*pairs):
        return [jnp.sum(first * second, axis=0) for first, second in pairs]

    mixed = exchange(mix(rhs))
    rhs_own, rhs_other = line_gather(rhs)
    tile_other = form(line_order(1), rows, cols, 512)
    tile_own = form(line_order(0), rows, cols, 512)
    other, sums_other = apply(tile_other, 512, order, mixed, [rhs_other])
    own, sums_own = apply(tile_own, 512, order, mixed, [rhs_own])
    norm_first, noise_first = local_sums((rhs, rhs), (rhs, noise_cols * rhs))
    curve_first = sums_own[0] + sums_other[0] + noise_first
    norm_first, curve_first = total_sums(jnp.stack([norm_first, curve_first]), samples)
    train, new_first = reduce_rows(own, other)
    image = mask * train + noise_cols * rhs
    step_first = norm_first / curve_first
    residual = rhs - spread(step_first) * image

    start = mix(residual)
    mixed = [exchange(start[:half]), exchange(start[half:])]
    res_own, res_other = line_gather(residual)

    def second(tile, tests):
        orders = order.reshape(2, -1) // 2
        width = items * plane // 2
        result, _ = apply(tile, 512, orders[0], mixed[0])
        return apply(tile, 512, orders[1], mixed[1], tests, result, width)

    other, sums_other = second(tile_other, [rhs_other, res_other])
    own, sums_own = second(tile_own, [rhs_own, res_own])
    tests = sums_own + sums_other
    norm_next, res_image, noise_rhs, noise_res = local_sums(
        (residual, residual),
        (residual, image),
        (rhs, noise_cols * residual),
        (residual, noise_cols * residual),
    )
    partial = jnp.stack([norm_next, res_image, tests[0] + noise_rhs, tests[1] + noise_res])
    norm_next, res_image, rhs_answer, res_answer = total_sums(partial, samples)
    ratio = norm_next / norm_first
    curve_second = res_answer + ratio * (res_image + rhs_answer + ratio * curve_first)
    step_second = norm_next / curve_second
    train, new_second = reduce_rows(own, other)
    answer = mask * train + noise_cols * residual
    residual = residual - spread(step_second) * (answer + spread(ratio) * image)
    predicted = (
        prior_new
        + spread(step_first + step_second * ratio) * new_first
        + spread(step_second) * new_second
    )
    return (residual, predicted)


def solution(mesh):
    return jax.shard_map(
        shards,
        mesh=mesh,
        in_specs=(
            P(("row", "col"), None),
            P(("row", "col"), None),
            P(("row", "col")),
            P(("row", "col"), None),
            P(("row", "col"), None),
            P(("row", "col"), None),
            P(("row", "col"), None),
            P(),
            P(),
        ),
        out_specs=(P(("row", "col"), None), P(("row", "col"), None)),
        check_vma=False,
    )
```

profile of v0, /device:TPU:0, one launch (start us, length us, event | category | flops | bytes accessed | tf_op | source)
XLA Modules:
  0.0 402.1 jit_solution(16986605658678962620)
XLA Ops:
  4.4 5.6 %all-to-all-start.1 = ((f32[8,320,256]{2,1,0:T(8,128)}), f32[8,320,256]{2,1,0:T(8,128)S(1)}, u32[]{:S(2)}, u32[]{:S(2)}) async-start(f32[8,320,256]{2,1,0:T(8,128)} %broadcast_in_dim.25), calls=%async_computation.1 | async-start | bytes 5242880 | tf_op jit(solution)/shard_map/all_to_all | solution.py:246
  15.7 27.1 %all-to-all-done.1.refs_11_ = f32[8,320,256]{2,1,0:T(8,128)S(1)} async-done(((f32[8,320,256]{2,1,0:T(8,128)}), f32[8,320,256]{2,1,0:T(8,128)S(1)}, u32[]{:S(2)}, u32[]{:S(2)}) %all-to-all-start.1) | async-done | bytes 2621472 | tf_op jit(solution)/shard_map/all_to_all | solution.py:246
  42.8 3.5 broadcast_in_dim.24
  46.3 7.1 %all-to-all-start = ((f32[16,256,256]{2,1,0:T(8,128)}), f32[16,256,256]{2,1,0:T(8,128)}, u32[]{:S(2)}, u32[]{:S(2)}) async-start(f32[16,256,256]{2,1,0:T(8,128)} %broadcast_in_dim.24), calls=%async_computation | async-start | bytes 8388608 | tf_op jit(solution)/shard_map/all_to_all | solution.py:265
  60.6 39.9 %collective-permute-done.12.refs_1_ = f32[128,256]{1,0:T(8,128)S(1)} collective-permute-done((f32[128,256]{1,0:T(8,128)S(1)}, f32[128,256]{1,0:T(8,128)S(1)}, u32[]{:S(2)}, u32[]{:S(2)}) %collective-permute-start.12) | collective-permute-done | bytes 131104 | tf_op jit(solution)/shard_map/ppermute | solution.py:27
  103.9 11.0 %collective-permute-done.4.refs_1_ = f32[128,256]{1,0:T(8,128)S(1)} collective-permute-done((f32[128,256]{1,0:T(8,128)S(1)}, f32[128,256]{1,0:T(8,128)S(1)}, u32[]{:S(2)}, u32[]{:S(2)}) %collective-permute-start.4) | collective-permute-done | bytes 131104 | tf_op jit(solution)/shard_map/ppermute | solution.py:27
  134.3 5.6 %collective-permute-done.2.refs_3_ = f32[128,256]{1,0:T(8,128)S(1)} collective-permute-done((f32[128,256]{1,0:T(8,128)S(1)}, f32[128,256]{1,0:T(8,128)S(1)}, u32[]{:S(2)}, u32[]{:S(2)}) %collective-permute-start.2) | collective-permute-done | bytes 131104 | tf_op jit(solution)/shard_map/ppermute | solution.py:27
  153.2 3.5 collective-permute-start.11
  162.1 17.8 %form.3 = (bf16[1280,4096]{1,0:T(8,128)(2,1)}, bf16[1280,4096]{1,0:T(8,128)(2,1)}) custom-call(s32[4]{0:T(128)} %get-tuple-element.64.refs_0_, f32[512,256]{1,0:T(8,128)} %join.5.refs_1_, f32[512,256]{1,0:T(8,128)} %collective-permute-done.8.refs_2_, f32[512,256]{1,0:T(8,128)} %collective-permute-done.9.refs_3_, f32[256,256]{1,0:T(8,128)} %collective-permute-done.10.refs_4_, ...), custom_call_target="tpu_custom_call" | custom-call | flops 8053063680 | bytes 20971520 | tf_op jit(solution)/shard_map/form/pallas_call | solution.py:148
  180.8 17.1 %apply.7 = (f32[1280,256]{1,0:T(8,128)}, f32[8,256]{1,0:T(8,128)}) custom-call(s32[32]{0:T(128)} %get-tuple-element.60.refs_0_, f32[32,128,256]{2,1,0:T(8,128)} %bitcast.3.refs_1_, f32[1024,256]{1,0:T(8,128)} %copy-done.7, bf16[1280,4096]{1,0:T(8,128)(2,1)} %get-tuple-element.19.refs_3_.refs_2_.refs_5_, ...), custom_call_target="tpu_custom_call" | custom-call | flops 8053063680 | bytes 20971520 | tf_op jit(solution)/shard_map/apply/pallas_call | solution.py:202
  198.0 17.3 %form.2 = (bf16[1280,4096]{1,0:T(8,128)(2,1)}, bf16[1280,4096]{1,0:T(8,128)(2,1)}) custom-call(s32[4]{0:T(128)} %get-tuple-element.63.refs_0_, f32[512,256]{1,0:T(8,128)} %join.5.refs_1_, f32[512,256]{1,0:T(8,128)} %collective-permute-done.8.refs_2_, f32[512,256]{1,0:T(8,128)} %collective-permute-done.9.refs_3_, f32[256,256]{1,0:T(8,128)} %collective-permute-done.10.refs_4_, ...), custom_call_target="tpu_custom_call" | custom-call | flops 8053063680 | bytes 20971520 | tf_op jit(solution)/shard_map/form/pallas_call | solution.py:148
  215.3 17.2 %apply.6 = (f32[1280,256]{1,0:T(8,128)}, f32[8,256]{1,0:T(8,128)}) custom-call(s32[32]{0:T(128)} %get-tuple-element.60.refs_0_, f32[32,128,256]{2,1,0:T(8,128)} %bitcast.3.refs_1_, f32[1024,256]{1,0:T(8,128)} %join.4.refs_2_.refs_3_, bf16[1280,4096]{1,0:T(8,128)(2,1)} %get-tuple-element.16.refs_3_.refs_2_.refs_5_, ...), custom_call_target="tpu_custom_call" | custom-call | flops 8053063680 | bytes 20971520 | tf_op jit(solution)/shard_map/apply/pallas_call | solution.py:202
  234.1 3.3 collective-permute-start.24
  238.9 7.1 %all-to-all-start.2 = ((f32[128,2,256]{2,1,0:T(2,128)}), f32[128,2,256]{2,1,0:T(2,128)S(1)}, u32[]{:S(2)}, u32[]{:S(2)}) async-start(f32[128,2,256]{2,1,0:T(2,128)} %broadcast_in_dim.26), calls=%async_computation.2 | async-start | bytes 524288 | tf_op jit(solution)/shard_map/all_to_all | solution.py:221
  249.7 7.2 %all-to-all-done.2 = f32[128,2,256]{2,1,0:T(2,128)S(1)} async-done(((f32[128,2,256]{2,1,0:T(2,128)}), f32[128,2,256]{2,1,0:T(2,128)S(1)}, u32[]{:S(2)}, u32[]{:S(2)}) %all-to-all-start.2) | async-done | bytes 262176 | tf_op jit(solution)/shard_map/all_to_all | solution.py:221
  263.7 33.1 %all_to_all.30.refs_1_ = f32[16,128,256]{2,1,0:T(8,128)} all-to-all(f32[16,128,256]{2,1,0:T(8,128)S(1)} %broadcast_in_dim.29), channel_id=1, replica_groups=mesh['row'=16,'col'=8] {'row'}, dimensions={0} | all-to-all | bytes 4194304 | tf_op jit(solution)/shard_map/all_to_all | solution.py:265
  298.4 3.7 all-to-all-start.3
  305.4 4.3 %collective-permute-done.26.refs_1_ = f32[256,256]{1,0:T(8,128)S(1)} collective-permute-done((f32[256,256]{1,0:T(8,128)S(1)}, f32[256,256]{1,0:T(8,128)S(1)}, u32[]{:S(2)}, u32[]{:S(2)}) %collective-permute-start.26) | collective-permute-done | bytes 262176 | tf_op jit(solution)/shard_map/ppermute | solution.py:27
  319.7 9.9 %apply.10 = (f32[1280,256]{1,0:T(8,128)}, f32[8,256]{1,0:T(8,128)}) custom-call(s32[16]{0:T(128)} %get-tuple-element.61.refs_0_, f32[16,128,256]{2,1,0:T(8,128)} %all_to_all.30.refs_1_, bf16[1280,4096]{1,0:T(8,128)(2,1)} %get-tuple-element.19.refs_3_.refs_2_.refs_5_, bf16[1280,4096]{1,0:T(8,128)(2,1)} %get-tuple-element.20.refs_4_.refs_3_.refs_6_), custom_call_target="tpu_custom_call" | custom-call | flops 4026531840 | bytes 10485760 | tf_op jit(solution)/shard_map/apply/pallas_call | solution.py:202
  331.2 11.2 %apply.11 = (f32[1280,256]{1,0:T(8,128)}, f32[8,256]{1,0:T(8,128)}) custom-call(s32[16]{0:T(128)} %get-tuple-element.62.refs_0_, f32[16,128,256]{2,1,0:T(8,128)} %copy-done, f32[1280,256]{1,0:T(8,128)} %get-tuple-element.26.refs_2_, f32[1024,256]{1,0:T(8,128)} %copy-done.7, f32[1024,256]{1,0:T(8,128)} %collective-permute-done.30.refs_4_, ...), custom_call_target="tpu_custom_call" | custom-call | flops 4026531840 | bytes 10485760 | tf_op jit(solution)/shard_map/apply/pallas_call | solution.py:202
  342.7 9.9 %apply.8 = (f32[1280,256]{1,0:T(8,128)}, f32[8,256]{1,0:T(8,128)}) custom-call(s32[16]{0:T(128)} %get-tuple-element.61.refs_0_, f32[16,128,256]{2,1,0:T(8,128)} %all_to_all.30.refs_1_, bf16[1280,4096]{1,0:T(8,128)(2,1)} %get-tuple-element.16.refs_3_.refs_2_.refs_5_, bf16[1280,4096]{1,0:T(8,128)(2,1)} %get-tuple-element.17.refs_4_.refs_3_.refs_6_), custom_call_target="tpu_custom_call" | custom-call | flops 4026531840 | bytes 10485760 | tf_op jit(solution)/shard_map/apply/pallas_call | solution.py:202
  352.6 11.3 %apply.9 = (f32[1280,256]{1,0:T(8,128)}, f32[8,256]{1,0:T(8,128)}) custom-call(s32[16]{0:T(128)} %get-tuple-element.62.refs_0_, f32[16,128,256]{2,1,0:T(8,128)} %copy-done, f32[1280,256]{1,0:T(8,128)} %get-tuple-element.24.refs_2_, f32[1024,256]{1,0:T(8,128)} %join.4.refs_2_.refs_3_, f32[1024,256]{1,0:T(8,128)} %join.7.refs_4_, ...), custom_call_target="tpu_custom_call" | custom-call | flops 4026531840 | bytes 10485760 | tf_op jit(solution)/shard_map/apply/pallas_call | solution.py:202
  371.9 9.2 %all-to-all-start.5 = ((f32[128,4,256]{2,1,0:T(4,128)}), f32[128,4,256]{2,1,0:T(4,128)S(1)}, u32[]{:S(2)}, u32[]{:S(2)}) async-start(f32[128,4,256]{2,1,0:T(4,128)} %broadcast_in_dim.30), calls=%async_computation.5 | async-start | bytes 1048576 | tf_op jit(solution)/shard_map/all_to_all | solution.py:221
  386.4 8.4 %all-to-all-done.5 = f32[128,4,256]{2,1,0:T(4,128)S(1)} async-done(((f32[128,4,256]{2,1,0:T(4,128)}), f32[128,4,256]{2,1,0:T(4,128)S(1)}, u32[]{:S(2)}, u32[]{:S(2)}) %all-to-all-start.5) | async-done | bytes 524320 | tf_op jit(solution)/shard_map/all_to_all | solution.py:221
  (217 shorter events, 109.7 us)
Async XLA Ops:
  4.4 38.3 %all-to-all-start.1 = ((f32[8,320,256]{2,1,0:T(8,128)}), f32[8,320,256]{2,1,0:T(8,128)S(1)}, u32[]{:S(2)}, u32[]{:S(2)}) async-start(f32[8,320,256]{2,1,0:T(8,128)} %broadcast_in_dim.25), calls=%async_computation.1 | async-start | bytes 5242880 | tf_op jit(solution)/shard_map/all_to_all | solution.py:246
  46.3 133.6 %all-to-all-start = ((f32[16,256,256]{2,1,0:T(8,128)}), f32[16,256,256]{2,1,0:T(8,128)}, u32[]{:S(2)}, u32[]{:S(2)}) async-start(f32[16,256,256]{2,1,0:T(8,128)} %broadcast_in_dim.24), calls=%async_computation | async-start | bytes 8388608 | tf_op jit(solution)/shard_map/all_to_all | solution.py:265
  53.4 76.7 %collective-permute-start = (f32[256,256]{1,0:T(8,128)S(1)}, f32[256,256]{1,0:T(8,128)S(1)}, u32[]{:S(2)}, u32[]{:S(2)}) collective-permute-start(f32[256,256]{1,0:T(8,128)S(1)} %get-tuple-element.40.refs_0_), channel_id=1, source_target_pairs={{0,2},{1,3},{2,4},{3,5},{4,6},{5,7},{6,0},{7,1},{8,10},{9,11},{10,... | collective-permute-start | bytes 786440 | tf_op jit(solution)/shard_map/ppermute | solution.py:27
  54.1 46.4 %collective-permute-start.12 = (f32[128,256]{1,0:T(8,128)S(1)}, f32[128,256]{1,0:T(8,128)S(1)}, u32[]{:S(2)}, u32[]{:S(2)}) collective-permute-start(f32[128,256]{1,0:T(8,128)S(1)} %get-tuple-element.53.refs_0_), channel_id=1, source_target_pairs={{0,8},{1,9},{2,10},{3,11},{4,12},{5,13},{6,14},{7,15},{8,16},{9,17... | collective-permute-start | bytes 393224 | tf_op jit(solution)/shard_map/ppermute | solution.py:27
  55.9 44.6 %collective-permute-start.13 = (f32[128,256]{1,0:T(8,128)S(1)}, f32[128,256]{1,0:T(8,128)S(1)}, u32[]{:S(2)}, u32[]{:S(2)}) collective-permute-start(f32[128,256]{1,0:T(8,128)S(1)} %get-tuple-element.53.refs_0_), channel_id=1, source_target_pairs={{0,24},{1,25},{2,26},{3,27},{4,28},{5,29},{6,30},{7,31},{8,0},{9,1... | collective-permute-start | bytes 393224 | tf_op jit(solution)/shard_map/ppermute | solution.py:27
  57.4 57.5 %collective-permute-start.4 = (f32[128,256]{1,0:T(8,128)S(1)}, f32[128,256]{1,0:T(8,128)S(1)}, u32[]{:S(2)}, u32[]{:S(2)}) collective-permute-start(f32[128,256]{1,0:T(8,128)S(1)} %get-tuple-element.54.refs_0_), channel_id=1, source_target_pairs={{0,32},{1,33},{2,34},{3,35},{4,36},{5,37},{6,38},{7,39},{8,40},{9,... | collective-permute-start | bytes 393224 | tf_op jit(solution)/shard_map/ppermute | solution.py:27
  59.2 58.3 %collective-permute-start.5 = (f32[128,256]{1,0:T(8,128)S(1)}, f32[128,256]{1,0:T(8,128)S(1)}, u32[]{:S(2)}, u32[]{:S(2)}) collective-permute-start(f32[128,256]{1,0:T(8,128)S(1)} %get-tuple-element.54.refs_0_), channel_id=1, source_target_pairs={{0,96},{1,97},{2,98},{3,99},{4,100},{5,101},{6,102},{7,103},{8,104... | collective-permute-start | bytes 393224 | tf_op jit(solution)/shard_map/ppermute | solution.py:27
  100.5 20.0 %collective-permute-start.14 = (f32[64,256]{1,0:T(8,128)S(1)}, f32[64,256]{1,0:T(8,128)S(1)}, u32[]{:S(2)}, u32[]{:S(2)}) collective-permute-start(f32[64,256]{1,0:T(8,128)S(1)} %slice.177), channel_id=1, source_target_pairs={{0,8},{1,9},{2,10},{3,11},{4,12},{5,13},{6,14},{7,15},{8,16},{9,17... | collective-permute-start | bytes 196616 | tf_op jit(solution)/shard_map/ppermute | solution.py:27
  100.6 21.1 %collective-permute-start.15 = (f32[64,256]{1,0:T(8,128)S(1)}, f32[64,256]{1,0:T(8,128)S(1)}, u32[]{:S(2)}, u32[]{:S(2)}) collective-permute-start(f32[64,256]{1,0:T(8,128)S(1)} %slice.178), channel_id=1, source_target_pairs={{0,24},{1,25},{2,26},{3,27},{4,28},{5,29},{6,30},{7,31},{8,0},{9,1... | collective-permute-start | bytes 196616 | tf_op jit(solution)/shard_map/ppermute | solution.py:27
  120.5 12.9 %collective-permute-start.1 = (f32[256,256]{1,0:T(8,128)S(1)}, f32[256,256]{1,0:T(8,128)S(1)}, u32[]{:S(2)}, u32[]{:S(2)}) collective-permute-start(f32[256,256]{1,0:T(8,128)S(1)} %get-tuple-element.40.refs_0_), channel_id=1, source_target_pairs={{0,6},{1,7},{2,0},{3,1},{4,2},{5,3},{6,4},{7,5},{8,14},{9,15},{10,... | collective-permute-start | bytes 786440 | tf_op jit(solution)/shard_map/ppermute | solution.py:27
  124.2 23.5 %collective-permute-start.16 = (f32[512,256]{1,0:T(8,128)}, f32[512,256]{1,0:T(8,128)S(1)}, u32[]{:S(2)}, u32[]{:S(2)}) collective-permute-start(f32[512,256]{1,0:T(8,128)} %join.6.refs_6_), channel_id=1, source_target_pairs={{0,32},{1,33},{2,34},{3,35},{4,36},{5,37},{6,38},{7,39},{8,40},{9,... | collective-permute-start | bytes 1572872 | tf_op jit(solution)/shard_map/ppermute | solution.py:27
  124.3 23.6 %collective-permute-start.17 = (f32[512,256]{1,0:T(8,128)}, f32[512,256]{1,0:T(8,128)S(1)}, u32[]{:S(2)}, u32[]{:S(2)}) collective-permute-start(f32[512,256]{1,0:T(8,128)} %join.6.refs_6_), channel_id=1, source_target_pairs={{0,96},{1,97},{2,98},{3,99},{4,100},{5,101},{6,102},{7,103},{8,104... | collective-permute-start | bytes 1572872 | tf_op jit(solution)/shard_map/ppermute | solution.py:27
  130.1 21.1 %collective-permute-start.8 = (f32[512,256]{1,0:T(8,128)}, f32[512,256]{1,0:T(8,128)}, u32[]{:S(2)}, u32[]{:S(2)}) collective-permute-start(f32[512,256]{1,0:T(8,128)} %join.5.refs_1_), channel_id=1, source_target_pairs={{0,8},{1,9},{2,10},{3,11},{4,12},{5,13},{6,14},{7,15},{8,16},{9,17... | collective-permute-start | bytes 1572872 | tf_op jit(solution)/shard_map/ppermute | solution.py:27
  130.1 22.2 %collective-permute-start.9 = (f32[512,256]{1,0:T(8,128)}, f32[512,256]{1,0:T(8,128)}, u32[]{:S(2)}, u32[]{:S(2)}) collective-permute-start(f32[512,256]{1,0:T(8,128)} %join.5.refs_1_), channel_id=1, source_target_pairs={{0,24},{1,25},{2,26},{3,27},{4,28},{5,29},{6,30},{7,31},{8,0},{9,1... | collective-permute-start | bytes 1572872 | tf_op jit(solution)/shard_map/ppermute | solution.py:27
  147.8 32.1 %collective-permute-start.20 = (f32[1024,256]{1,0:T(8,128)}, f32[1024,256]{1,0:T(8,128)S(1)}, u32[]{:S(2)}, u32[]{:S(2)}) collective-permute-start(f32[1024,256]{1,0:T(8,128)} %join.4.refs_2_.refs_3_), channel_id=1, source_target_pairs={{0,1},{1,0},{2,3},{3,2},{4,5},{5,4},{6,7},{7,6},{8,9},{9,8},{10,11... | collective-permute-start | bytes 3145736 | tf_op jit(solution)/shard_map/ppermute | solution.py:27
  198.0 34.5 %collective-permute-start.21 = (f32[1280,256]{1,0:T(8,128)}, f32[1280,256]{1,0:T(8,128)S(1)}, u32[]{:S(2)}, u32[]{:S(2)}) collective-permute-start(f32[1280,256]{1,0:T(8,128)} %get-tuple-element.23), channel_id=1, source_target_pairs={{0,1},{1,0},{2,3},{3,2},{4,5},{5,4},{6,7},{7,6},{8,9},{9,8},{10,11... | collective-permute-start | bytes 3932168 | tf_op jit(solution)/shard_map/ppermute | solution.py:27
  238.9 18.0 %all-to-all-start.2 = ((f32[128,2,256]{2,1,0:T(2,128)}), f32[128,2,256]{2,1,0:T(2,128)S(1)}, u32[]{:S(2)}, u32[]{:S(2)}) async-start(f32[128,2,256]{2,1,0:T(2,128)} %broadcast_in_dim.26), calls=%async_computation.2 | async-start | bytes 524288 | tf_op jit(solution)/shard_map/all_to_all | solution.py:221
  298.4 31.5 %all-to-all-start.3 = ((f32[16,128,256]{2,1,0:T(8,128)}), f32[16,128,256]{2,1,0:T(8,128)S(1)}, u32[]{:S(2)}, u32[]{:S(2)}) async-start(f32[16,128,256]{2,1,0:T(8,128)} %broadcast_in_dim.28), calls=%async_computation.3 | async-start | bytes 4194304 | tf_op jit(solution)/shard_map/all_to_all | solution.py:265
  342.4 22.2 %collective-permute-start.31 = (f32[1280,256]{1,0:T(8,128)}, f32[1280,256]{1,0:T(8,128)S(1)}, u32[]{:S(2)}, u32[]{:S(2)}) collective-permute-start(f32[1280,256]{1,0:T(8,128)} %get-tuple-element.29), channel_id=1, source_target_pairs={{0,1},{1,0},{2,3},{3,2},{4,5},{5,4},{6,7},{7,6},{8,9},{9,8},{10,11... | collective-permute-start | bytes 3932168 | tf_op jit(solution)/shard_map/ppermute | solution.py:27
  367.7 13.4 %collective-permute-start.32 = (f32[160,256]{1,0:T(8,128)S(1)}, f32[160,256]{1,0:T(8,128)S(1)}, u32[]{:S(2)}, u32[]{:S(2)}) collective-permute-start(f32[160,256]{1,0:T(8,128)S(1)} %get-tuple-element.44), channel_id=1, source_target_pairs={{0,2},{1,3},{2,4},{3,5},{4,6},{5,7},{6,0},{7,1},{8,10},{9,11},{10,... | collective-permute-start | bytes 491528 | tf_op jit(solution)/shard_map/ppermute | solution.py:27
  369.0 12.1 %collective-permute-start.34 = (f32[160,256]{1,0:T(8,128)S(1)}, f32[160,256]{1,0:T(8,128)}, u32[]{:S(2)}, u32[]{:S(2)}) collective-permute-start(f32[160,256]{1,0:T(8,128)S(1)} %get-tuple-element.42), channel_id=1, source_target_pairs={{0,6},{1,7},{2,0},{3,1},{4,2},{5,3},{6,4},{7,5},{8,14},{9,15},{10,... | collective-permute-start | bytes 491528 | tf_op jit(solution)/shard_map/ppermute | solution.py:27
  371.9 22.9 %all-to-all-start.5 = ((f32[128,4,256]{2,1,0:T(4,128)}), f32[128,4,256]{2,1,0:T(4,128)S(1)}, u32[]{:S(2)}, u32[]{:S(2)}) async-start(f32[128,4,256]{2,1,0:T(4,128)} %broadcast_in_dim.30), calls=%async_computation.5 | async-start | bytes 1048576 | tf_op jit(solution)/shard_map/all_to_all | solution.py:221
  382.8 13.8 %collective-permute-start.35 = (f32[320,256]{1,0:T(8,128)}, f32[320,256]{1,0:T(8,128)S(1)}, u32[]{:S(2)}, u32[]{:S(2)}) collective-permute-start(f32[320,256]{1,0:T(8,128)} %pad_maximum_fusion.3), channel_id=1, source_target_pairs={{0,6},{1,7},{2,0},{3,1},{4,2},{5,3},{6,4},{7,5},{8,14},{9,15},{10,... | collective-permute-start | bytes 983048 | tf_op jit(solution)/shard_map/ppermute | solution.py:27
  386.4 13.2 %collective-permute-start.33 = (f32[320,256]{1,0:T(8,128)}, f32[320,256]{1,0:T(8,128)}, u32[]{:S(2)}, u32[]{:S(2)}) collective-permute-start(f32[320,256]{1,0:T(8,128)} %pad_maximum_fusion.2), channel_id=1, source_target_pairs={{0,2},{1,3},{2,4},{3,5},{4,6},{5,7},{6,0},{7,1},{8,10},{9,11},{10,... | collective-permute-start | bytes 983048 | tf_op jit(solution)/shard_map/ppermute | solution.py:27
  (51 other events, 669.3 us)
where the time goes:
time: 404 us; the launch traced here: 402 us
  waiting for transfers between devices  120 us (30%)
  Pallas kernels  120 us (30%)
  starting transfers between devices  85.6 us (21%)
  blocking collectives  33.1 us (8%)
  local copies, waits for them, and re-layouts  25.6 us (6%)
  other arithmetic  14.8 us (4%)
    ppermute x36, waiting for transfers between devices, shift(): return lax.ppermute(values, AXES, pairs)  77.3 us
    pallas_call x6, Pallas kernels, apply(): pl.pallas_call(lambda *refs: apply_kernel(len(tests), before is not None,...  76.6 us
    ppermute x36, starting transfers between devices, shift(): return lax.ppermute(values, AXES, pairs)  53 us
    pallas_call x2, Pallas kernels, form(): pl.pallas_call(lambda *refs: form_kernel(len(cols), *refs), grid_spec=plt...  35.1 us
    all_to_all x1, blocking collectives, exchange(): received = lax.all_to_all(spread_out, 'row', 0, 0)  33.1 us
    all_to_all x1, waiting for transfers between devices, shards(): lax.all_to_all(jnp.broadcast_to(normed[None], (line,) + normed.shape), 'c...  27.1 us
    all_to_all x2, starting transfers between devices, total_sums(): sums = jnp.sum(lax.all_to_all(spread, AXES, 0, 0), axis=0)  16.3 us
    all_to_all x2, waiting for transfers between devices, total_sums(): sums = jnp.sum(lax.all_to_all(spread, AXES, 0, 0), axis=0)  15.6 us
  transfers between devices with their start and end apart: 41, of which 16 were waited for; matrix products, arithmetic and copies ran while one was open for 5% of the time, Pallas kernels for 23%

commit v1 on v0

--- a/solution.py
+++ b/solution.py
@@ -250,7 +250,7 @@
     mixing = jnp.kron(jnp.eye(samples, dtype=F32), time_kernel)
 
     def mix(values):
-        return jnp.dot(values, mixing, precision=lax.Precision.HIGHEST)
+        return jnp.dot(values, mixing, precision=lax.Precision.HIGH)
 
     position = jnp.arange(columns, dtype=jnp.int32) % checkpoints
     mask = (position[None, :] < lengths[:, None]).astype(F32)
@@ -289,7 +289,7 @@
     rhs_own, rhs_other = line_gather(rhs)
     tile_other = form(line_order(1), rows, cols, 512)
     tile_own = form(line_order(0), rows, cols, 512)
-    other, sums_other = apply(tile_other, 512, order, mixed, [rhs_other])
+    other, sums_other = apply(tile_other, 1024, order, mixed, [rhs_other])
     own, sums_own = apply(tile_own, 512, order, mixed, [rhs_own])
     norm_first, noise_first = local_sums((rhs, rhs), (rhs, noise_cols * rhs))
     curve_first = sums_own[0] + sums_other[0] + noise_first
@@ -306,7 +306,7 @@
     def second(tile, tests):
         orders = order.reshape(2, -1) // 2
         width = items * plane // 2
-        result, _ = apply(tile, 512, orders[0], mixed[0])
+        result, _ = apply(tile, 256, orders[0], mixed[0])
         return apply(tile, 512, orders[1], mixed[1], tests, result, width)
 
     other, sums_other = second(tile_other, [rhs_other, res_other])

time: 404 us -> 407 us (level)
  transfers between devices with their start and end apart: 41 -> 41, of which waited for: 16 -> 15; matrix products, arithmetic and copies ran while one was open for 5% -> 5% of each run, Pallas kernels for 23% -> 24%
where the time goes in v1:
time: 407 us; the launch traced here: 405 us
  Pallas kernels  123 us (30%)
  waiting for transfers between devices  120 us (29%)
  starting transfers between devices  86.3 us (21%)
  blocking collectives  33.1 us (8%)
  local copies, waits for them, and re-layouts  25.6 us (6%)
  other arithmetic  14.8 us (4%)
    pallas_call x6, Pallas kernels, apply(): pl.pallas_call(lambda *refs: apply_kernel(len(tests), before is not None,...  79.2 us
    ppermute x36, waiting for transfers between devices, shift(): return lax.ppermute(values, AXES, pairs)  77.3 us
    ppermute x36, starting transfers between devices, shift(): return lax.ppermute(values, AXES, pairs)  53.2 us
    pallas_call x2, Pallas kernels, form(): pl.pallas_call(lambda *refs: form_kernel(len(cols), *refs), grid_spec=plt...  35.1 us
    all_to_all x1, blocking collectives, exchange(): received = lax.all_to_all(spread_out, 'row', 0, 0)  33.1 us
    all_to_all x1, waiting for transfers between devices, shards(): lax.all_to_all(jnp.broadcast_to(normed[None], (line,) + normed.shape), 'c...  27.2 us
    all_to_all x2, starting transfers between devices, total_sums(): sums = jnp.sum(lax.all_to_all(spread, AXES, 0, 0), axis=0)  16.5 us
    all_to_all x2, waiting for transfers between devices, total_sums(): sums = jnp.sum(lax.all_to_all(spread, AXES, 0, 0), axis=0)  15.6 us
  transfers between devices with their start and end apart: 41, of which 15 were waited for; matrix products, arithmetic and copies ran while one was open for 5% of the time, Pallas kernels for 24%

profile of v1, /device:TPU:0, one launch (start us, length us, event | category | flops | bytes accessed | tf_op | source)
XLA Modules:
  0.0 405.0 jit_solution(8700004313910085720)
XLA Ops:
  4.4 5.6 %all-to-all-start.1 = ((f32[8,320,256]{2,1,0:T(8,128)}), f32[8,320,256]{2,1,0:T(8,128)S(1)}, u32[]{:S(2)}, u32[]{:S(2)}) async-start(f32[8,320,256]{2,1,0:T(8,128)} %broadcast_in_dim.25), calls=%async_computation.1 | async-start | bytes 5242880 | tf_op jit(solution)/shard_map/all_to_all | solution.py:246
  15.6 27.2 %all-to-all-done.1.refs_11_ = f32[8,320,256]{2,1,0:T(8,128)S(1)} async-done(((f32[8,320,256]{2,1,0:T(8,128)}), f32[8,320,256]{2,1,0:T(8,128)S(1)}, u32[]{:S(2)}, u32[]{:S(2)}) %all-to-all-start.1) | async-done | bytes 2621472 | tf_op jit(solution)/shard_map/all_to_all | solution.py:246
  42.8 3.5 broadcast_in_dim.24
  46.3 7.1 %all-to-all-start = ((f32[16,256,256]{2,1,0:T(8,128)}), f32[16,256,256]{2,1,0:T(8,128)}, u32[]{:S(2)}, u32[]{:S(2)}) async-start(f32[16,256,256]{2,1,0:T(8,128)} %broadcast_in_dim.24), calls=%async_computation | async-start | bytes 8388608 | tf_op jit(solution)/shard_map/all_to_all | solution.py:265
  60.6 39.9 %collective-permute-done.12.refs_1_ = f32[128,256]{1,0:T(8,128)S(1)} collective-permute-done((f32[128,256]{1,0:T(8,128)S(1)}, f32[128,256]{1,0:T(8,128)S(1)}, u32[]{:S(2)}, u32[]{:S(2)}) %collective-permute-start.12) | collective-permute-done | bytes 131104 | tf_op jit(solution)/shard_map/ppermute | solution.py:27
  103.9 11.0 %collective-permute-done.4.refs_1_ = f32[128,256]{1,0:T(8,128)S(1)} collective-permute-done((f32[128,256]{1,0:T(8,128)S(1)}, f32[128,256]{1,0:T(8,128)S(1)}, u32[]{:S(2)}, u32[]{:S(2)}) %collective-permute-start.4) | collective-permute-done | bytes 131104 | tf_op jit(solution)/shard_map/ppermute | solution.py:27
  134.3 5.6 %collective-permute-done.2.refs_3_ = f32[128,256]{1,0:T(8,128)S(1)} collective-permute-done((f32[128,256]{1,0:T(8,128)S(1)}, f32[128,256]{1,0:T(8,128)S(1)}, u32[]{:S(2)}, u32[]{:S(2)}) %collective-permute-start.2) | collective-permute-done | bytes 131104 | tf_op jit(solution)/shard_map/ppermute | solution.py:27
  153.2 3.5 collective-permute-start.11
  162.1 17.8 %form.3 = (bf16[1280,4096]{1,0:T(8,128)(2,1)}, bf16[1280,4096]{1,0:T(8,128)(2,1)}) custom-call(s32[4]{0:T(128)} %get-tuple-element.64.refs_0_, f32[512,256]{1,0:T(8,128)} %join.5.refs_1_, f32[512,256]{1,0:T(8,128)} %collective-permute-done.8.refs_2_, f32[512,256]{1,0:T(8,128)} %collective-permute-done.9.refs_3_, f32[256,256]{1,0:T(8,128)} %collective-permute-done.10.refs_4_, ...), custom_call_target="tpu_custom_call" | custom-call | flops 8053063680 | bytes 20971520 | tf_op jit(solution)/shard_map/form/pallas_call | solution.py:148
  180.8 15.5 %apply.7 = (f32[1280,256]{1,0:T(8,128)}, f32[8,256]{1,0:T(8,128)}) custom-call(s32[32]{0:T(128)} %get-tuple-element.60.refs_0_, f32[32,128,256]{2,1,0:T(8,128)} %bitcast.3.refs_1_, f32[1024,256]{1,0:T(8,128)} %copy-done.7, bf16[1280,4096]{1,0:T(8,128)(2,1)} %get-tuple-element.19.refs_3_.refs_2_.refs_5_, ...), custom_call_target="tpu_custom_call" | custom-call | flops 8053063680 | bytes 20971520 | tf_op jit(solution)/shard_map/apply/pallas_call | solution.py:202
  196.4 17.3 %form.2 = (bf16[1280,4096]{1,0:T(8,128)(2,1)}, bf16[1280,4096]{1,0:T(8,128)(2,1)}) custom-call(s32[4]{0:T(128)} %get-tuple-element.63.refs_0_, f32[512,256]{1,0:T(8,128)} %join.5.refs_1_, f32[512,256]{1,0:T(8,128)} %collective-permute-done.8.refs_2_, f32[512,256]{1,0:T(8,128)} %collective-permute-done.9.refs_3_, f32[256,256]{1,0:T(8,128)} %collective-permute-done.10.refs_4_, ...), custom_call_target="tpu_custom_call" | custom-call | flops 8053063680 | bytes 20971520 | tf_op jit(solution)/shard_map/form/pallas_call | solution.py:148
  213.7 17.2 %apply.6 = (f32[1280,256]{1,0:T(8,128)}, f32[8,256]{1,0:T(8,128)}) custom-call(s32[32]{0:T(128)} %get-tuple-element.60.refs_0_, f32[32,128,256]{2,1,0:T(8,128)} %bitcast.3.refs_1_, f32[1024,256]{1,0:T(8,128)} %join.4.refs_2_.refs_3_, bf16[1280,4096]{1,0:T(8,128)(2,1)} %get-tuple-element.16.refs_3_.refs_2_.refs_5_, ...), custom_call_target="tpu_custom_call" | custom-call | flops 8053063680 | bytes 20971520 | tf_op jit(solution)/shard_map/apply/pallas_call | solution.py:202
  232.5 3.3 collective-permute-start.24
  237.3 7.1 %all-to-all-start.2 = ((f32[128,2,256]{2,1,0:T(2,128)}), f32[128,2,256]{2,1,0:T(2,128)S(1)}, u32[]{:S(2)}, u32[]{:S(2)}) async-start(f32[128,2,256]{2,1,0:T(2,128)} %broadcast_in_dim.26), calls=%async_computation.2 | async-start | bytes 524288 | tf_op jit(solution)/shard_map/all_to_all | solution.py:221
  248.1 7.2 %all-to-all-done.2 = f32[128,2,256]{2,1,0:T(2,128)S(1)} async-done(((f32[128,2,256]{2,1,0:T(2,128)}), f32[128,2,256]{2,1,0:T(2,128)S(1)}, u32[]{:S(2)}, u32[]{:S(2)}) %all-to-all-start.2) | async-done | bytes 262176 | tf_op jit(solution)/shard_map/all_to_all | solution.py:221
  262.0 33.1 %all_to_all.30.refs_1_ = f32[16,128,256]{2,1,0:T(8,128)} all-to-all(f32[16,128,256]{2,1,0:T(8,128)S(1)} %broadcast_in_dim.29), channel_id=1, replica_groups=mesh['row'=16,'col'=8] {'row'}, dimensions={0} | all-to-all | bytes 4194304 | tf_op jit(solution)/shard_map/all_to_all | solution.py:265
  296.7 3.9 all-to-all-start.3
  303.9 4.3 %collective-permute-done.26.refs_1_ = f32[256,256]{1,0:T(8,128)S(1)} collective-permute-done((f32[256,256]{1,0:T(8,128)S(1)}, f32[256,256]{1,0:T(8,128)S(1)}, u32[]{:S(2)}, u32[]{:S(2)}) %collective-permute-start.26) | collective-permute-done | bytes 262176 | tf_op jit(solution)/shard_map/ppermute | solution.py:27
  318.2 12.0 %apply.10 = (f32[1280,256]{1,0:T(8,128)}, f32[8,256]{1,0:T(8,128)}) custom-call(s32[16]{0:T(128)} %get-tuple-element.61.refs_0_, f32[16,128,256]{2,1,0:T(8,128)} %all_to_all.30.refs_1_, bf16[1280,4096]{1,0:T(8,128)(2,1)} %get-tuple-element.19.refs_3_.refs_2_.refs_5_, bf16[1280,4096]{1,0:T(8,128)(2,1)} %get-tuple-element.20.refs_4_.refs_3_.refs_6_), custom_call_target="tpu_custom_call" | custom-call | flops 4026531840 | bytes 10485760 | tf_op jit(solution)/shard_map/apply/pallas_call | solution.py:202
  331.6 11.2 %apply.11 = (f32[1280,256]{1,0:T(8,128)}, f32[8,256]{1,0:T(8,128)}) custom-call(s32[16]{0:T(128)} %get-tuple-element.62.refs_0_, f32[16,128,256]{2,1,0:T(8,128)} %copy-done, f32[1280,256]{1,0:T(8,128)} %get-tuple-element.26.refs_2_, f32[1024,256]{1,0:T(8,128)} %copy-done.7, f32[1024,256]{1,0:T(8,128)} %collective-permute-done.30.refs_4_, ...), custom_call_target="tpu_custom_call" | custom-call | flops 4026531840 | bytes 10485760 | tf_op jit(solution)/shard_map/apply/pallas_call | solution.py:202
  343.3 12.0 %apply.8 = (f32[1280,256]{1,0:T(8,128)}, f32[8,256]{1,0:T(8,128)}) custom-call(s32[16]{0:T(128)} %get-tuple-element.61.refs_0_, f32[16,128,256]{2,1,0:T(8,128)} %all_to_all.30.refs_1_, bf16[1280,4096]{1,0:T(8,128)(2,1)} %get-tuple-element.16.refs_3_.refs_2_.refs_5_, bf16[1280,4096]{1,0:T(8,128)(2,1)} %get-tuple-element.17.refs_4_.refs_3_.refs_6_), custom_call_target="tpu_custom_call" | custom-call | flops 4026531840 | bytes 10485760 | tf_op jit(solution)/shard_map/apply/pallas_call | solution.py:202
  355.3 11.3 %apply.9 = (f32[1280,256]{1,0:T(8,128)}, f32[8,256]{1,0:T(8,128)}) custom-call(s32[16]{0:T(128)} %get-tuple-element.62.refs_0_, f32[16,128,256]{2,1,0:T(8,128)} %copy-done, f32[1280,256]{1,0:T(8,128)} %get-tuple-element.24.refs_2_, f32[1024,256]{1,0:T(8,128)} %join.4.refs_2_.refs_3_, f32[1024,256]{1,0:T(8,128)} %join.7.refs_4_, ...), custom_call_target="tpu_custom_call" | custom-call | flops 4026531840 | bytes 10485760 | tf_op jit(solution)/shard_map/apply/pallas_call | solution.py:202
  374.6 9.4 %all-to-all-start.5 = ((f32[128,4,256]{2,1,0:T(4,128)}), f32[128,4,256]{2,1,0:T(4,128)S(1)}, u32[]{:S(2)}, u32[]{:S(2)}) async-start(f32[128,4,256]{2,1,0:T(4,128)} %broadcast_in_dim.30), calls=%async_computation.5 | async-start | bytes 1048576 | tf_op jit(solution)/shard_map/all_to_all | solution.py:221
  389.3 8.4 %all-to-all-done.5 = f32[128,4,256]{2,1,0:T(4,128)S(1)} async-done(((f32[128,4,256]{2,1,0:T(4,128)}), f32[128,4,256]{2,1,0:T(4,128)S(1)}, u32[]{:S(2)}, u32[]{:S(2)}) %all-to-all-start.5) | async-done | bytes 524320 | tf_op jit(solution)/shard_map/all_to_all | solution.py:221
  (217 shorter events, 109.4 us)
Async XLA Ops:
  4.4 38.3 %all-to-all-start.1 = ((f32[8,320,256]{2,1,0:T(8,128)}), f32[8,320,256]{2,1,0:T(8,128)S(1)}, u32[]{:S(2)}, u32[]{:S(2)}) async-start(f32[8,320,256]{2,1,0:T(8,128)} %broadcast_in_dim.25), calls=%async_computation.1 | async-start | bytes 5242880 | tf_op jit(solution)/shard_map/all_to_all | solution.py:246
  46.3 133.6 %all-to-all-start = ((f32[16,256,256]{2,1,0:T(8,128)}), f32[16,256,256]{2,1,0:T(8,128)}, u32[]{:S(2)}, u32[]{:S(2)}) async-start(f32[16,256,256]{2,1,0:T(8,128)} %broadcast_in_dim.24), calls=%async_computation | async-start | bytes 8388608 | tf_op jit(solution)/shard_map/all_to_all | solution.py:265
  53.4 76.7 %collective-permute-start = (f32[256,256]{1,0:T(8,128)S(1)}, f32[256,256]{1,0:T(8,128)S(1)}, u32[]{:S(2)}, u32[]{:S(2)}) collective-permute-start(f32[256,256]{1,0:T(8,128)S(1)} %get-tuple-element.40.refs_0_), channel_id=1, source_target_pairs={{0,2},{1,3},{2,4},{3,5},{4,6},{5,7},{6,0},{7,1},{8,10},{9,11},{10,... | collective-permute-start | bytes 786440 | tf_op jit(solution)/shard_map/ppermute | solution.py:27
  54.1 46.4 %collective-permute-start.12 = (f32[128,256]{1,0:T(8,128)S(1)}, f32[128,256]{1,0:T(8,128)S(1)}, u32[]{:S(2)}, u32[]{:S(2)}) collective-permute-start(f32[128,256]{1,0:T(8,128)S(1)} %get-tuple-element.53.refs_0_), channel_id=1, source_target_pairs={{0,8},{1,9},{2,10},{3,11},{4,12},{5,13},{6,14},{7,15},{8,16},{9,17... | collective-permute-start | bytes 393224 | tf_op jit(solution)/shard_map/ppermute | solution.py:27
  55.9 44.6 %collective-permute-start.13 = (f32[128,256]{1,0:T(8,128)S(1)}, f32[128,256]{1,0:T(8,128)S(1)}, u32[]{:S(2)}, u32[]{:S(2)}) collective-permute-start(f32[128,256]{1,0:T(8,128)S(1)} %get-tuple-element.53.refs_0_), channel_id=1, source_target_pairs={{0,24},{1,25},{2,26},{3,27},{4,28},{5,29},{6,30},{7,31},{8,0},{9,1... | collective-permute-start | bytes 393224 | tf_op jit(solution)/shard_map/ppermute | solution.py:27
  57.4 57.5 %collective-permute-start.4 = (f32[128,256]{1,0:T(8,128)S(1)}, f32[128,256]{1,0:T(8,128)S(1)}, u32[]{:S(2)}, u32[]{:S(2)}) collective-permute-start(f32[128,256]{1,0:T(8,128)S(1)} %get-tuple-element.54.refs_0_), channel_id=1, source_target_pairs={{0,32},{1,33},{2,34},{3,35},{4,36},{5,37},{6,38},{7,39},{8,40},{9,... | collective-permute-start | bytes 393224 | tf_op jit(solution)/shard_map/ppermute | solution.py:27
  59.2 58.3 %collective-permute-start.5 = (f32[128,256]{1,0:T(8,128)S(1)}, f32[128,256]{1,0:T(8,128)S(1)}, u32[]{:S(2)}, u32[]{:S(2)}) collective-permute-start(f32[128,256]{1,0:T(8,128)S(1)} %get-tuple-element.54.refs_0_), channel_id=1, source_target_pairs={{0,96},{1,97},{2,98},{3,99},{4,100},{5,101},{6,102},{7,103},{8,104... | collective-permute-start | bytes 393224 | tf_op jit(solution)/shard_map/ppermute | solution.py:27
  100.5 20.0 %collective-permute-start.14 = (f32[64,256]{1,0:T(8,128)S(1)}, f32[64,256]{1,0:T(8,128)S(1)}, u32[]{:S(2)}, u32[]{:S(2)}) collective-permute-start(f32[64,256]{1,0:T(8,128)S(1)} %slice.177), channel_id=1, source_target_pairs={{0,8},{1,9},{2,10},{3,11},{4,12},{5,13},{6,14},{7,15},{8,16},{9,17... | collective-permute-start | bytes 196616 | tf_op jit(solution)/shard_map/ppermute | solution.py:27
  100.6 21.1 %collective-permute-start.15 = (f32[64,256]{1,0:T(8,128)S(1)}, f32[64,256]{1,0:T(8,128)S(1)}, u32[]{:S(2)}, u32[]{:S(2)}) collective-permute-start(f32[64,256]{1,0:T(8,128)S(1)} %slice.178), channel_id=1, source_target_pairs={{0,24},{1,25},{2,26},{3,27},{4,28},{5,29},{6,30},{7,31},{8,0},{9,1... | collective-permute-start | bytes 196616 | tf_op jit(solution)/shard_map/ppermute | solution.py:27
  120.5 12.9 %collective-permute-start.1 = (f32[256,256]{1,0:T(8,128)S(1)}, f32[256,256]{1,0:T(8,128)S(1)}, u32[]{:S(2)}, u32[]{:S(2)}) collective-permute-start(f32[256,256]{1,0:T(8,128)S(1)} %get-tuple-element.40.refs_0_), channel_id=1, source_target_pairs={{0,6},{1,7},{2,0},{3,1},{4,2},{5,3},{6,4},{7,5},{8,14},{9,15},{10,... | collective-permute-start | bytes 786440 | tf_op jit(solution)/shard_map/ppermute | solution.py:27
  124.2 23.5 %collective-permute-start.16 = (f32[512,256]{1,0:T(8,128)}, f32[512,256]{1,0:T(8,128)S(1)}, u32[]{:S(2)}, u32[]{:S(2)}) collective-permute-start(f32[512,256]{1,0:T(8,128)} %join.6.refs_6_), channel_id=1, source_target_pairs={{0,32},{1,33},{2,34},{3,35},{4,36},{5,37},{6,38},{7,39},{8,40},{9,... | collective-permute-start | bytes 1572872 | tf_op jit(solution)/shard_map/ppermute | solution.py:27
  124.3 23.6 %collective-permute-start.17 = (f32[512,256]{1,0:T(8,128)}, f32[512,256]{1,0:T(8,128)S(1)}, u32[]{:S(2)}, u32[]{:S(2)}) collective-permute-start(f32[512,256]{1,0:T(8,128)} %join.6.refs_6_), channel_id=1, source_target_pairs={{0,96},{1,97},{2,98},{3,99},{4,100},{5,101},{6,102},{7,103},{8,104... | collective-permute-start | bytes 1572872 | tf_op jit(solution)/shard_map/ppermute | solution.py:27
  130.1 21.1 %collective-permute-start.8 = (f32[512,256]{1,0:T(8,128)}, f32[512,256]{1,0:T(8,128)}, u32[]{:S(2)}, u32[]{:S(2)}) collective-permute-start(f32[512,256]{1,0:T(8,128)} %join.5.refs_1_), channel_id=1, source_target_pairs={{0,8},{1,9},{2,10},{3,11},{4,12},{5,13},{6,14},{7,15},{8,16},{9,17... | collective-permute-start | bytes 1572872 | tf_op jit(solution)/shard_map/ppermute | solution.py:27
  130.1 22.2 %collective-permute-start.9 = (f32[512,256]{1,0:T(8,128)}, f32[512,256]{1,0:T(8,128)}, u32[]{:S(2)}, u32[]{:S(2)}) collective-permute-start(f32[512,256]{1,0:T(8,128)} %join.5.refs_1_), channel_id=1, source_target_pairs={{0,24},{1,25},{2,26},{3,27},{4,28},{5,29},{6,30},{7,31},{8,0},{9,1... | collective-permute-start | bytes 1572872 | tf_op jit(solution)/shard_map/ppermute | solution.py:27
  147.8 32.1 %collective-permute-start.20 = (f32[1024,256]{1,0:T(8,128)}, f32[1024,256]{1,0:T(8,128)S(1)}, u32[]{:S(2)}, u32[]{:S(2)}) collective-permute-start(f32[1024,256]{1,0:T(8,128)} %join.4.refs_2_.refs_3_), channel_id=1, source_target_pairs={{0,1},{1,0},{2,3},{3,2},{4,5},{5,4},{6,7},{7,6},{8,9},{9,8},{10,11... | collective-permute-start | bytes 3145736 | tf_op jit(solution)/shard_map/ppermute | solution.py:27
  196.4 34.5 %collective-permute-start.21 = (f32[1280,256]{1,0:T(8,128)}, f32[1280,256]{1,0:T(8,128)S(1)}, u32[]{:S(2)}, u32[]{:S(2)}) collective-permute-start(f32[1280,256]{1,0:T(8,128)} %get-tuple-element.23), channel_id=1, source_target_pairs={{0,1},{1,0},{2,3},{3,2},{4,5},{5,4},{6,7},{7,6},{8,9},{9,8},{10,11... | collective-permute-start | bytes 3932168 | tf_op jit(solution)/shard_map/ppermute | solution.py:27
  237.3 18.0 %all-to-all-start.2 = ((f32[128,2,256]{2,1,0:T(2,128)}), f32[128,2,256]{2,1,0:T(2,128)S(1)}, u32[]{:S(2)}, u32[]{:S(2)}) async-start(f32[128,2,256]{2,1,0:T(2,128)} %broadcast_in_dim.26), calls=%async_computation.2 | async-start | bytes 524288 | tf_op jit(solution)/shard_map/all_to_all | solution.py:221
  296.7 33.6 %all-to-all-start.3 = ((f32[16,128,256]{2,1,0:T(8,128)}), f32[16,128,256]{2,1,0:T(8,128)S(1)}, u32[]{:S(2)}, u32[]{:S(2)}) async-start(f32[16,128,256]{2,1,0:T(8,128)} %broadcast_in_dim.28), calls=%async_computation.3 | async-start | bytes 4194304 | tf_op jit(solution)/shard_map/all_to_all | solution.py:265
  342.8 24.5 %collective-permute-start.31 = (f32[1280,256]{1,0:T(8,128)}, f32[1280,256]{1,0:T(8,128)S(1)}, u32[]{:S(2)}, u32[]{:S(2)}) collective-permute-start(f32[1280,256]{1,0:T(8,128)} %get-tuple-element.29), channel_id=1, source_target_pairs={{0,1},{1,0},{2,3},{3,2},{4,5},{5,4},{6,7},{7,6},{8,9},{9,8},{10,11... | collective-permute-start | bytes 3932168 | tf_op jit(solution)/shard_map/ppermute | solution.py:27
  370.3 13.7 %collective-permute-start.32 = (f32[160,256]{1,0:T(8,128)S(1)}, f32[160,256]{1,0:T(8,128)S(1)}, u32[]{:S(2)}, u32[]{:S(2)}) collective-permute-start(f32[160,256]{1,0:T(8,128)S(1)} %get-tuple-element.44), channel_id=1, source_target_pairs={{0,2},{1,3},{2,4},{3,5},{4,6},{5,7},{6,0},{7,1},{8,10},{9,11},{10,... | collective-permute-start | bytes 491528 | tf_op jit(solution)/shard_map/ppermute | solution.py:27
  370.4 13.6 %collective-permute-start.34 = (f32[160,256]{1,0:T(8,128)S(1)}, f32[160,256]{1,0:T(8,128)}, u32[]{:S(2)}, u32[]{:S(2)}) collective-permute-start(f32[160,256]{1,0:T(8,128)S(1)} %get-tuple-element.42), channel_id=1, source_target_pairs={{0,6},{1,7},{2,0},{3,1},{4,2},{5,3},{6,4},{7,5},{8,14},{9,15},{10,... | collective-permute-start | bytes 491528 | tf_op jit(solution)/shard_map/ppermute | solution.py:27
  374.6 23.1 %all-to-all-start.5 = ((f32[128,4,256]{2,1,0:T(4,128)}), f32[128,4,256]{2,1,0:T(4,128)S(1)}, u32[]{:S(2)}, u32[]{:S(2)}) async-start(f32[128,4,256]{2,1,0:T(4,128)} %broadcast_in_dim.30), calls=%async_computation.5 | async-start | bytes 1048576 | tf_op jit(solution)/shard_map/all_to_all | solution.py:221
  385.7 13.8 %collective-permute-start.35 = (f32[320,256]{1,0:T(8,128)}, f32[320,256]{1,0:T(8,128)S(1)}, u32[]{:S(2)}, u32[]{:S(2)}) collective-permute-start(f32[320,256]{1,0:T(8,128)} %pad_maximum_fusion.3), channel_id=1, source_target_pairs={{0,6},{1,7},{2,0},{3,1},{4,2},{5,3},{6,4},{7,5},{8,14},{9,15},{10,... | collective-permute-start | bytes 983048 | tf_op jit(solution)/shard_map/ppermute | solution.py:27
  389.3 13.2 %collective-permute-start.33 = (f32[320,256]{1,0:T(8,128)}, f32[320,256]{1,0:T(8,128)}, u32[]{:S(2)}, u32[]{:S(2)}) collective-permute-start(f32[320,256]{1,0:T(8,128)} %pad_maximum_fusion.2), channel_id=1, source_target_pairs={{0,2},{1,3},{2,4},{3,5},{4,6},{5,7},{6,0},{7,1},{8,10},{9,11},{10,... | collective-permute-start | bytes 983048 | tf_op jit(solution)/shard_map/ppermute | solution.py:27
  (51 other events, 671.5 us)
